TPU v7x, 32 devices: a whole 2x2x4 slice. The times are simulated.
32 devices in a mesh: dp: 4 (over z), expert: 8 (over y, x, core).
Axes of the slice: x: 2, y: 2, z: 4, core: 2. Of those that a mesh axis runs over, the one named last changes fastest.
Arguments:
- tokens: bfloat16 [8192, 1280], P(('dp', 'expert')), may hold values from -14 to 14
- ln_gain: float32 [1280], replicated, may hold values from 0.25 to 1.75
- router: bfloat16 [1280, 8], replicated, may hold values from -0.3125 to 0.3125
- w_in: bfloat16 [8, 5120, 1280], P('expert', 'dp'), may hold values from -0.15625 to 0.15625
- b_in: bfloat16 [8, 5120], P('expert', 'dp'), may hold values from -3 to 3
- w_out: bfloat16 [8, 5120, 1280], P('expert', 'dp'), may hold values from -0.078125 to 0.078125
- b_out: bfloat16 [8, 1280], P('expert'), may hold values from -3 to 3
- expert_choice: int32 [8192], P(('dp', 'expert')), may hold values from 0 to 7
- modality: int32 [8192], P(('dp', 'expert')), may hold values from 0 to 1, as said below
- slot: int32 [8192], P(('dp', 'expert')), may hold values from -1 to 15, as said below
Outputs:
- moe_out: bfloat16 [8192, 1280], P(('dp', 'expert'))
- aux_losses: float32 [2, 2], replicated
Inputs may be any that keep to these rules, and one draw needn't show every extreme that they name: Each source's tokens with one expert and a slot other than -1 have distinct slots, numbered from 0 in token order; one expert has all 16 slots filled in every source. `modality`: every source holds tokens of both modalities.
All inputs are finite; a program needn't handle non-finite values.
Results may differ from a plain program's by a relative error of at most 0.007.
Values may be sent and summed in bfloat16 or wider, within the bound.
No kernel may reach another device: no remote copies, remote signals or barrier semaphores. Data moves between devices by JAX's collectives and lax.ppermute only.
A program may use at most 128 MiB of HBM per device.

v0:
```python
import jax
import jax.numpy as jnp
from jax import lax
from jax.sharding import PartitionSpec as P

CAP = 16


def layer_norm(tokens, ln_gain):
    values = tokens.astype(jnp.float32)
    center = values - jnp.mean(values, axis=-1, keepdims=True)
    spread = jnp.mean(center * center, axis=-1, keepdims=True)
    return (center * lax.rsqrt(spread + 1e-06) * ln_gain).astype(jnp.bfloat16)


def expert_hidden(rows, first, first_bias, second):
    pre = lax.dot_general(rows, first, (((1,), (1,)), ((), ())), preferred_element_type=jnp.float32)
    hidden = jax.nn.gelu(pre + first_bias.astype(jnp.float32), approximate=False).astype(
        jnp.bfloat16
    )
    return jnp.dot(hidden, second, preferred_element_type=jnp.float32)


def on_device(tokens, ln_gain, router, w_in, b_in, w_out, b_out, expert_choice, modality, slot):
    normed = layer_norm(tokens, ln_gain)
    logits = jnp.dot(normed, router, preferred_element_type=jnp.float32)
    logp = jax.nn.log_softmax(logits, axis=-1)
    probs = jnp.exp(logp)
    gate = jnp.take_along_axis(probs, expert_choice[:, None], axis=1)[:, 0]
    experts_all = router.shape[1]
    width = normed.shape[1]
    columns = experts_all * CAP
    target = jnp.where(slot >= 0, expert_choice * CAP + slot, -1)
    table = (target[:, None] == jnp.arange(columns, dtype=jnp.int32)[None, :]).astype(jnp.bfloat16)
    buffer = jnp.einsum("tk,td->kd", table, normed, preferred_element_type=jnp.float32).astype(
        jnp.bfloat16
    )
    received = lax.all_to_all(
        buffer.reshape(experts_all, CAP, width), "expert", split_axis=0, concat_axis=0, tiled=True
    )
    senders = lax.axis_size("expert")
    local_count = w_in.shape[0]
    received = received.reshape(senders, local_count, CAP, width)
    rows = received[:, 0].reshape(senders * CAP, width)
    gathered = lax.all_gather(rows, "dp", axis=0, tiled=True)
    summed = lax.psum_scatter(
        expert_hidden(gathered, w_in[0], b_in[0], w_out[0]), "dp", scatter_dimension=0, tiled=True
    )
    results = [
        (summed + b_out[0].astype(jnp.float32)).astype(jnp.bfloat16).reshape(senders, CAP, width)
    ]
    outputs = jnp.stack(results, axis=1).reshape(experts_all, CAP, width)
    returned = lax.all_to_all(outputs, "expert", split_axis=0, concat_axis=0, tiled=True)
    fetched = jnp.dot(table, returned.reshape(columns, width), preferred_element_type=jnp.float32)
    moe_out = (gate[:, None] * fetched).astype(jnp.bfloat16)
    textual = (modality == 1).astype(jnp.float32)
    select = jnp.stack([1.0 - textual, textual], axis=0)
    entropy = -jnp.sum(probs * logp, axis=-1)
    prob_part = jnp.dot(select, probs, precision=lax.Precision.HIGHEST)
    ent_part = jnp.dot(select, entropy, precision=lax.Precision.HIGHEST)
    count_part = jnp.sum(select, axis=1)
    prob_sum, ent_sum, count = lax.psum((prob_part, ent_part, count_part), ("dp", "expert"))
    pbar = prob_sum / count[:, None]
    aux_losses = jnp.stack([ent_sum / count, jnp.sum(pbar * jnp.log(pbar), axis=1)], axis=1)
    return (moe_out, aux_losses)


def solution(mesh):
    return jax.shard_map(
        on_device,
        mesh=mesh,
        in_specs=(
            P(("dp", "expert"), None),
            P(),
            P(),
            P("expert", "dp", None),
            P("expert", "dp"),
            P("expert", "dp", None),
            P("expert", None),
            P(("dp", "expert")),
            P(("dp", "expert")),
            P(("dp", "expert")),
        ),
        out_specs=(P(("dp", "expert"), None), P()),
        check_vma=False,
    )
```

profile of v0, /device:TPU:0, one launch (start us, length us, event | category | flops | bytes accessed | tf_op | source)
XLA Modules:
  0.0 144.7 jit_solution(16310733744528008156)
XLA Ops:
  7.2 0.0 all-gather.2.cloned.1.call-start
  7.3 1.4 convert_reduce_fusion
  8.7 1.4 fusion.18
  10.1 1.4 fusion.20
  11.5 0.8 copy-done.1
  12.3 0.4 convolution_convert_fusion
  12.7 12.7 %all_to_all.10 = bf16[8,16,1280]{2,1,0:T(8,128)(2,1)} all-to-all(bf16[8,16,1280]{2,1,0:T(8,128)(2,1)S(1)} %bitcast.35), channel_id=1, replica_groups=mesh['dp'=4,'expert'=8] {'expert'}, dimensions={0} | all-to-all | bytes 655360 | tf_op jit(solution)/shard_map/all_to_all | solution.py:38
  25.4 0.0 reduce-scatter.2.cloned.1.call-start
  25.5 32.0 %all-gather.2.cloned.1.call-done = bf16[512,1280]{1,0:T(8,128)(2,1)} async-done(((bf16[128,1280]{1,0:T(8,128)(2,1)}), bf16[512,1280]{1,0:T(8,128)(2,1)}) %all-gather.2.cloned.1.call-update) | async-done | bytes 1310736 | tf_op jit(solution)/shard_map/all_gather | solution.py:45
  57.5 12.3 %fusion = f32[512,1280]{1,0:T(8,128)} fusion(bf16[1,1280,1280]{2,1,0:T(8,128)(2,1)S(1)} %copy-done, bf16[512,1280]{1,0:T(8,128)(2,1)} %all-gather.2.cloned.1.call-done, bf16[1,1280,1280]{2,1,0:T(8,128)(2,1)} %param.13, f32[1280]{0:T(1024)S(1)} %convert_reduce_fusion.2), kind=kOutput, calls=%fused_computation.3 | convolution fusion | flops 3398696960 | bytes 10490880 | tf_op jit(solution)/shard_map/dot_general | solution.py:21
  69.8 0.7 copy-done.2
  70.5 1.4 fusion.61
  72.0 0.1 convolution_bitcast_fusion
  72.1 0.1 fusion.29
  72.3 0.1 fusion.60
  72.4 41.3 %all-reduce = (f32[2,8]{1,0:T(2,128)S(1)}, f32[2]{0:T(128)S(1)}, f32[2]{0:T(128)S(1)}) all-reduce(f32[2,8]{1,0:T(2,128)S(1)} %fusion.29, f32[2]{0:T(128)S(1)} %fusion.60, f32[2]{0:T(128)S(1)} %convolution_bitcast_fusion), channel_id=1, replica_groups=mesh['dp'=4,'expert'=8] {'dp','expert'}, use_global_device_ids=true, to_apply=%region_9.10 | all-reduce | flops 20 | bytes 160 | tf_op jit(solution)/shard_map/psum | solution.py:62
  113.7 0.2 fusion.25
  114.0 8.2 %reduce-scatter.2.cloned.1.call-done = f32[128,1280]{1,0:T(8,128)} async-done(((f32[512,1280]{1,0:T(8,128)}), f32[128,1280]{1,0:T(8,128)}) %reduce-scatter.2.cloned.1.call-update) | async-done | bytes 655376 | tf_op jit(solution)/shard_map/reduce_scatter | solution.py:46
  122.1 1.9 %add_convert_fusion = bf16[128,1280]{1,0:T(8,128)(2,1)} fusion(f32[128,1280]{1,0:T(8,128)} %reduce-scatter.2.cloned.1.call-done, f32[1280]{0:T(1024)S(1)} %convert_reduce_fusion.1), kind=kLoop, calls=%fused_computation.35 | loop fusion | flops 327680 | bytes 988160 | tf_op jit(solution)/shard_map/convert_element_type | solution.py:50
  124.0 4.1 %all-to-all-start.1 = ((bf16[8,16,1280]{2,1,0:T(8,128)(2,1)}), bf16[8,16,1280]{2,1,0:T(8,128)(2,1)}, u32[]{:S(2)}, u32[]{:S(2)}) async-start(bf16[8,16,1280]{2,1,0:T(8,128)(2,1)} %bitcast.33), calls=%async_computation.2 | async-start | bytes 655360 | tf_op jit(solution)/shard_map/all_to_all | solution.py:53
  128.1 0.6 copy.14
  128.7 1.8 %gather_fusion = f32[256]{0:T(256)S(1)} fusion(f32[256,8]{0,1:T(8,128)S(1)} %get-tuple-element.12, s32[256]{0:T(256)S(1)} %bitcast.32), kind=kCustom, calls=%fused_computation | custom fusion | bytes 4096 | tf_op jit(solution)/shard_map/jit(take_along_axis)/gather | solution.py:29
  130.6 5.1 %all-to-all-done.1 = bf16[8,16,1280]{2,1,0:T(8,128)(2,1)} async-done(((bf16[8,16,1280]{2,1,0:T(8,128)(2,1)}), bf16[8,16,1280]{2,1,0:T(8,128)(2,1)}, u32[]{:S(2)}, u32[]{:S(2)}) %all-to-all-start.1) | async-done | bytes 327712 | tf_op jit(solution)/shard_map/all_to_all | solution.py:53
  135.7 2.2 %fusion.15 = bf16[256,1280]{1,0:T(8,128)(2,1)} fusion(bf16[128,1280]{1,0:T(8,128)(2,1)} %bitcast.8, f32[256]{0:T(256)S(1)} %and_select_fusion, s32[256]{0:T(256)S(1)} %get-tuple-element.14), kind=kOutput, calls=%fused_computation.25 | convolution fusion | flops 84574208 | bytes 985088 | tf_op jit(solution)/shard_map/dot_general | solution.py:54
  (33 shorter events, 0.2 us)
Async XLA Ops:
  7.2 50.3 %copy-start = (bf16[1,1280,1280]{2,1,0:T(8,128)(2,1)S(1)}, bf16[1,1280,1280]{2,1,0:T(8,128)(2,1)}, u32[]{:S(2)}) copy-start(bf16[1,1280,1280]{2,1,0:T(8,128)(2,1)} %param.15) | copy-start | bytes 9830404
  7.2 4.3 %copy-start.6 = (s32[256]{0:T(256)S(1)}, s32[256]{0:T(256)}, u32[]{:S(2)}) copy-start(s32[256]{0:T(256)} %param.17) | copy-start | bytes 3076
  7.2 4.3 %copy-start.7 = (s32[256]{0:T(256)S(1)}, s32[256]{0:T(256)}, u32[]{:S(2)}) copy-start(s32[256]{0:T(256)} %param.19) | copy-start | bytes 3076
  7.2 18.3 %copy-start.3 = (bf16[1,1280]{1,0:T(2,128)(2,1)S(1)}, bf16[1,1280]{1,0:T(2,128)(2,1)}, u32[]{:S(2)}) copy-start(bf16[1,1280]{1,0:T(2,128)(2,1)} %param.14) | copy-start | bytes 7684
  7.2 50.2 %all-gather.2.cloned.1.call-start = ((), (), s32[]{:S(2)}) async-start(), calls=%async_computation.3 | async-start | bytes 1638400 | tf_op jit(solution)/shard_map/all_gather | solution.py:45
  11.5 0.8 copy-start.1
  25.4 96.7 %reduce-scatter.2.cloned.1.call-start = ((), (), s32[]{:S(2)}) async-start(), calls=%async_computation.4 | async-start | bytes 3276800 | tf_op jit(solution)/shard_map/reduce_scatter | solution.py:46
  69.8 0.7 copy-start.2
  69.8 2.2 %copy-start.5 = (s32[256]{0:T(256)S(1)}, s32[256]{0:T(256)}, u32[]{:S(2)}) copy-start(s32[256]{0:T(256)} %param.18) | copy-start | bytes 3076
  69.8 44.0 %copy-start.4 = (bf16[1,1280]{1,0:T(2,128)(2,1)S(1)}, bf16[1,1280]{1,0:T(2,128)(2,1)}, u32[]{:S(2)}) copy-start(bf16[1,1280]{1,0:T(2,128)(2,1)} %param.16) | copy-start | bytes 7684
  124.0 11.7 %all-to-all-start.1 = ((bf16[8,16,1280]{2,1,0:T(8,128)(2,1)}), bf16[8,16,1280]{2,1,0:T(8,128)(2,1)}, u32[]{:S(2)}, u32[]{:S(2)}) async-start(bf16[8,16,1280]{2,1,0:T(8,128)(2,1)} %bitcast.33), calls=%async_computation.2 | async-start | bytes 655360 | tf_op jit(solution)/shard_map/all_to_all | solution.py:53
Sparse Core Ops, SparseCore 0:
  25.5 31.8 all-gather.1
  69.9 52.1 reduce-scatter.1
where the time goes:
time: 145 us
  blocking collectives  54 us (37%)
  waiting for transfers between devices  45.3 us (31%)
  matrix products  16.5 us (11%)
  between operations  14.3 us (10%)
  other arithmetic  6.49 us (4%)
  starting transfers between devices  4.15 us (3%)
  local copies, waits for them, and re-layouts  4.02 us (3%)
    psum x1, blocking collectives, on_device(): lax.psum((prob_part, ent_part, count_part), ('dp', 'expert'))  41.3 us
    all_gather x1, waiting for transfers between devices, on_device(): gathered = lax.all_gather(rows, 'dp', axis=0, tiled=True)  32 us
    all_to_all x1, blocking collectives, on_device(): lax.all_to_all(buffer.reshape(experts_all, CAP, width), 'expert', split_a...  12.7 us
    dot_general x1, matrix products, expert_hidden(): return jnp.dot(hidden, second, preferred_element_type=jnp.float32)  12.3 us
    reduce_scatter x1, waiting for transfers between devices, on_device(): lax.psum_scatter(expert_hidden(gathered, w_in[0], b_in[0], w_out[0]), 'dp...  8.17 us
    all_to_all x1, waiting for transfers between devices, on_device(): lax.all_to_all(outputs, 'expert', split_axis=0, concat_axis=0, tiled=True)  5.12 us
    all_to_all x1, starting transfers between devices, on_device(): lax.all_to_all(outputs, 'expert', split_axis=0, concat_axis=0, tiled=True)  4.07 us
  transfers between devices with their start and end apart: 3, of which 3 were waited for; matrix products, arithmetic and copies ran while one was open for 3% of the time, Pallas kernels for 0%

commit v1 on v0

--- a/solution.py
+++ b/solution.py
@@ -4,6 +4,11 @@
 from jax.sharding import PartitionSpec as P
 
 CAP = 16
+
+
+def one_after_other(array, inner_axis, outer_axis):
+    inner = lax.psum(array, inner_axis)
+    return lax.psum(inner, outer_axis)
 
 
 def layer_norm(tokens, ln_gain):
@@ -59,7 +64,7 @@
     prob_part = jnp.dot(select, probs, precision=lax.Precision.HIGHEST)
     ent_part = jnp.dot(select, entropy, precision=lax.Precision.HIGHEST)
     count_part = jnp.sum(select, axis=1)
-    prob_sum, ent_sum, count = lax.psum((prob_part, ent_part, count_part), ("dp", "expert"))
+    prob_sum, ent_sum, count = one_after_other((prob_part, ent_part, count_part), "expert", "dp")
     pbar = prob_sum / count[:, None]
     aux_losses = jnp.stack([ent_sum / count, jnp.sum(pbar * jnp.log(pbar), axis=1)], axis=1)
     return (moe_out, aux_losses)

time: 145 us -> 145 us (level)
  blocking collectives: 54 us -> 36.9 us
  waiting for transfers between devices: 45.3 us -> 61.7 us
    psum x1 -> x2, blocking collectives: 41.3 us -> 24.2 us  [the longest x1 12.9 us: one_after_other(): inner = lax.psum(array, inner_axis)]
    reduce_scatter x1, waiting for transfers between devices: 8.17 us -> 24.6 us  [on_device(): lax.psum_scatter(expert_hidden(gathered, w_in[0], b_in[0], w_out[0]), 'dp...]
where the time goes in v1:
time: 145 us; the launch traced here: 144 us
  waiting for transfers between devices  61.7 us (43%)
  blocking collectives  36.9 us (25%)
  matrix products  16.5 us (11%)
  between operations  14.3 us (10%)
  other arithmetic  6.49 us (4%)
  starting transfers between devices  4.15 us (3%)
  local copies, waits for them, and re-layouts  4.02 us (3%)
    all_gather x1, waiting for transfers between devices, on_device(): gathered = lax.all_gather(rows, 'dp', axis=0, tiled=True)  32 us
    reduce_scatter x1, waiting for transfers between devices, on_device(): lax.psum_scatter(expert_hidden(gathered, w_in[0], b_in[0], w_out[0]), 'dp...  24.6 us
    psum x1, blocking collectives, one_after_other(): inner = lax.psum(array, inner_axis)  12.9 us
    all_to_all x1, blocking collectives, on_device(): lax.all_to_all(buffer.reshape(experts_all, CAP, width), 'expert', split_a...  12.7 us
    dot_general x1, matrix products, expert_hidden(): return jnp.dot(hidden, second, preferred_element_type=jnp.float32)  12.3 us
    psum x1, blocking collectives, one_after_other(): return lax.psum(inner, outer_axis)  11.3 us
    all_to_all x1, waiting for transfers between devices, on_device(): lax.all_to_all(outputs, 'expert', split_axis=0, concat_axis=0, tiled=True)  5.12 us
    all_to_all x1, starting transfers between devices, on_device(): lax.all_to_all(outputs, 'expert', split_axis=0, concat_axis=0, tiled=True)  4.07 us
  transfers between devices with their start and end apart: 3, of which 3 were waited for; matrix products, arithmetic and copies ran while one was open for 3% of the time, Pallas kernels for 0%

profile of v1, /device:TPU:0, one launch (start us, length us, event | category | flops | bytes accessed | tf_op | source)
XLA Modules:
  0.0 144.1 jit_solution(17298223870674617863)
XLA Ops:
  7.3 1.4 convert_reduce_fusion
  8.7 1.4 fusion.18
  10.1 1.4 fusion.20
  11.5 0.8 copy-done.1
  12.3 0.4 convolution_convert_fusion
  12.7 12.7 %all_to_all.10 = bf16[8,16,1280]{2,1,0:T(8,128)(2,1)} all-to-all(bf16[8,16,1280]{2,1,0:T(8,128)(2,1)S(1)} %bitcast.35), channel_id=1, replica_groups=mesh['dp'=4,'expert'=8] {'expert'}, dimensions={0} | all-to-all | bytes 655360 | tf_op jit(solution)/shard_map/all_to_all | solution.py:43
  25.4 0.0 reduce-scatter.2.cloned.1.call-start
  25.5 32.0 %all-gather.2.cloned.1.call-done = bf16[512,1280]{1,0:T(8,128)(2,1)} async-done(((bf16[128,1280]{1,0:T(8,128)(2,1)}), bf16[512,1280]{1,0:T(8,128)(2,1)}) %all-gather.2.cloned.1.call-update) | async-done | bytes 1310736 | tf_op jit(solution)/shard_map/all_gather | solution.py:50
  57.5 12.3 %fusion = f32[512,1280]{1,0:T(8,128)} fusion(bf16[1,1280,1280]{2,1,0:T(8,128)(2,1)S(1)} %copy-done, bf16[512,1280]{1,0:T(8,128)(2,1)} %all-gather.2.cloned.1.call-done, bf16[1,1280,1280]{2,1,0:T(8,128)(2,1)} %param.13, f32[1280]{0:T(1024)S(1)} %convert_reduce_fusion.2), kind=kOutput, calls=%fused_computation.3 | convolution fusion | flops 3398696960 | bytes 10490880 | tf_op jit(solution)/shard_map/dot_general | solution.py:26
  69.8 0.7 copy-done.2
  70.5 1.4 fusion.61
  72.0 0.1 convolution_bitcast_fusion
  72.1 0.1 fusion.29
  72.3 0.1 fusion.60
  72.4 12.9 %all-reduce = (f32[2,8]{1,0:T(2,128)S(1)}, f32[2]{0:T(128)S(1)}, f32[2]{0:T(128)S(1)}) all-reduce(f32[2,8]{1,0:T(2,128)S(1)} %fusion.29, f32[2]{0:T(128)S(1)} %fusion.60, f32[2]{0:T(128)S(1)} %convolution_bitcast_fusion), channel_id=1, replica_groups=mesh['dp'=4,'expert'=8] {'expert'}, use_global_device_ids=true, to_apply=%region_11.12 | all-reduce | flops 20 | bytes 160 | tf_op jit(solution)/shard_map/psum | solution.py:10
  85.4 11.3 %all-reduce.1 = (f32[2,8]{1,0:T(2,128)S(1)}, f32[2]{0:T(128)S(1)}, f32[2]{0:T(128)S(1)}) all-reduce(f32[2,8]{1,0:T(2,128)S(1)} %get-tuple-element.8, f32[2]{0:T(128)S(1)} %get-tuple-element.9, f32[2]{0:T(128)S(1)} %get-tuple-element.10), channel_id=1, replica_groups=mesh['dp'=4,'expert'=8] {'dp'}, use_global_device_ids=true, to_apply=%region_12.13 | all-reduce | flops 20 | bytes 160 | tf_op jit(solution)/shard_map/psum | solution.py:11
  96.7 0.2 fusion.25
  96.9 24.6 %reduce-scatter.2.cloned.1.call-done = f32[128,1280]{1,0:T(8,128)} async-done(((f32[512,1280]{1,0:T(8,128)}), f32[128,1280]{1,0:T(8,128)}) %reduce-scatter.2.cloned.1.call-update) | async-done | bytes 655376 | tf_op jit(solution)/shard_map/reduce_scatter | solution.py:51
  121.5 1.9 %add_convert_fusion = bf16[128,1280]{1,0:T(8,128)(2,1)} fusion(f32[128,1280]{1,0:T(8,128)} %reduce-scatter.2.cloned.1.call-done, f32[1280]{0:T(1024)S(1)} %convert_reduce_fusion.1), kind=kLoop, calls=%fused_computation.35 | loop fusion | flops 327680 | bytes 988160 | tf_op jit(solution)/shard_map/convert_element_type | solution.py:55
  123.3 4.1 %all-to-all-start.1 = ((bf16[8,16,1280]{2,1,0:T(8,128)(2,1)}), bf16[8,16,1280]{2,1,0:T(8,128)(2,1)}, u32[]{:S(2)}, u32[]{:S(2)}) async-start(bf16[8,16,1280]{2,1,0:T(8,128)(2,1)} %bitcast.33), calls=%async_computation.2 | async-start | bytes 655360 | tf_op jit(solution)/shard_map/all_to_all | solution.py:58
  127.4 0.6 copy.14
  128.1 1.8 %gather_fusion = f32[256]{0:T(256)S(1)} fusion(f32[256,8]{0,1:T(8,128)S(1)} %get-tuple-element.15, s32[256]{0:T(256)S(1)} %bitcast.32), kind=kCustom, calls=%fused_computation | custom fusion | bytes 4096 | tf_op jit(solution)/shard_map/jit(take_along_axis)/gather | solution.py:34
  129.9 5.1 %all-to-all-done.1 = bf16[8,16,1280]{2,1,0:T(8,128)(2,1)} async-done(((bf16[8,16,1280]{2,1,0:T(8,128)(2,1)}), bf16[8,16,1280]{2,1,0:T(8,128)(2,1)}, u32[]{:S(2)}, u32[]{:S(2)}) %all-to-all-start.1) | async-done | bytes 327712 | tf_op jit(solution)/shard_map/all_to_all | solution.py:58
  135.0 2.2 %fusion.15 = bf16[256,1280]{1,0:T(8,128)(2,1)} fusion(bf16[128,1280]{1,0:T(8,128)(2,1)} %bitcast.8, f32[256]{0:T(256)S(1)} %and_select_fusion, s32[256]{0:T(256)S(1)} %get-tuple-element.17), kind=kOutput, calls=%fused_computation.25 | convolution fusion | flops 84574208 | bytes 985088 | tf_op jit(solution)/shard_map/dot_general | solution.py:59
  (34 shorter events, 0.3 us)
Async XLA Ops:
  7.2 50.3 %copy-start = (bf16[1,1280,1280]{2,1,0:T(8,128)(2,1)S(1)}, bf16[1,1280,1280]{2,1,0:T(8,128)(2,1)}, u32[]{:S(2)}) copy-start(bf16[1,1280,1280]{2,1,0:T(8,128)(2,1)} %param.15) | copy-start | bytes 9830404
  7.2 4.3 %copy-start.6 = (s32[256]{0:T(256)S(1)}, s32[256]{0:T(256)}, u32[]{:S(2)}) copy-start(s32[256]{0:T(256)} %param.17) | copy-start | bytes 3076
  7.2 4.3 %copy-start.7 = (s32[256]{0:T(256)S(1)}, s32[256]{0:T(256)}, u32[]{:S(2)}) copy-start(s32[256]{0:T(256)} %param.19) | copy-start | bytes 3076
  7.2 18.3 %copy-start.3 = (bf16[1,1280]{1,0:T(2,128)(2,1)S(1)}, bf16[1,1280]{1,0:T(2,128)(2,1)}, u32[]{:S(2)}) copy-start(bf16[1,1280]{1,0:T(2,128)(2,1)} %param.14) | copy-start | bytes 7684
  7.2 50.2 %all-gather.2.cloned.1.call-start = ((), (), s32[]{:S(2)}) async-start(), calls=%async_computation.3 | async-start | bytes 1638400 | tf_op jit(solution)/shard_map/all_gather | solution.py:50
  11.5 0.8 copy-start.1
  25.4 96.1 %reduce-scatter.2.cloned.1.call-start = ((), (), s32[]{:S(2)}) async-start(), calls=%async_computation.4 | async-start | bytes 3276800 | tf_op jit(solution)/shard_map/reduce_scatter | solution.py:51
  69.8 0.7 copy-start.2
  69.8 2.2 %copy-start.5 = (s32[256]{0:T(256)S(1)}, s32[256]{0:T(256)}, u32[]{:S(2)}) copy-start(s32[256]{0:T(256)} %param.18) | copy-start | bytes 3076
  69.8 26.9 %copy-start.4 = (bf16[1,1280]{1,0:T(2,128)(2,1)S(1)}, bf16[1,1280]{1,0:T(2,128)(2,1)}, u32[]{:S(2)}) copy-start(bf16[1,1280]{1,0:T(2,128)(2,1)} %param.16) | copy-start | bytes 7684
  123.3 11.7 %all-to-all-start.1 = ((bf16[8,16,1280]{2,1,0:T(8,128)(2,1)}), bf16[8,16,1280]{2,1,0:T(8,128)(2,1)}, u32[]{:S(2)}, u32[]{:S(2)}) async-start(bf16[8,16,1280]{2,1,0:T(8,128)(2,1)} %bitcast.33), calls=%async_computation.2 | async-start | bytes 655360 | tf_op jit(solution)/shard_map/all_to_all | solution.py:58
Sparse Core Ops, SparseCore 0:
  25.5 31.8 all-gather.1
  69.9 51.5 reduce-scatter.1
